TPU v7x, 128 devices: a whole 4x4x4 slice. The times are simulated.
128 devices in a mesh: lat: 16 (over x_lo, z, core), lon: 8 (over y, x_hi).
Axes of the slice: x: 4 (x_hi: 2, x_lo: 2; x = x_hi * 2 + x_lo), y: 4, z: 4, core: 2. Of those that a mesh axis runs over, the one named last changes fastest.
Arguments:
- forcing: float32 [16, 2048, 2048], P(None, 'lat', 'lon'), may hold values from -6 to 6
- metric_lon: float32 [2048, 2048], P('lat', 'lon'), may hold values from -0.5 to 0.5
- metric_lat: float32 [2048, 2048], P('lat', 'lon'), may hold values from -0.5 to 0.5
- lon_weights: float32 [2048], P('lon'), may hold values from 0.5 to 2
- eigen_basis: float32 [2048, 2048], replicated, may hold values from -0.125 to 0.125
- lower_mult: float32 [16, 2048, 2048], P('lon', 'lat'), may hold values from -1 to 0
- pivot_inverse: float32 [16, 2048, 2048], P('lon', 'lat'), may hold values from 0 to 2
- upper_coef: float32 [16, 2048, 2048], P('lon', 'lat'), may hold values from -33554432 to 0
Outputs:
- solution: float32 [16, 2048, 2048], P(None, 'lat', 'lon')
All inputs are finite; a program needn't handle non-finite values.
Results may differ from a plain program's by a relative error of at most 0.000082.
Values sent between devices are 32-bit elements; how exact they have to be, the bound alone decides.
A program may use at most 128 MiB of HBM per device.

v0:
```python
import jax
import jax.numpy as jnp
from jax import lax
from jax.sharding import PartitionSpec as P


def padded(shard, sides, width, wrap):
    for axis, dim in sides:
        count, length = (lax.axis_size(axis), shard.shape[dim])
        up = [(i, (i + 1) % count) for i in range(count if wrap else count - 1)]
        down = [(j, i) for i, j in up]
        last = lax.slice_in_dim(shard, length - width, length, axis=dim)
        initial = lax.slice_in_dim(shard, 0, width, axis=dim)
        before = lax.ppermute(last, axis, up)
        after = lax.ppermute(initial, axis, down)
        shard = jnp.concatenate([before, shard, after], axis=dim)
    return shard


def copy_for_each(shard, axis):
    count = lax.axis_size(axis)
    return lax.all_to_all(
        jnp.broadcast_to(shard[None], (count, *shard.shape)), axis, 0, 0, tiled=True
    )


def gathered_once(shard, axis):
    leaves = jax.tree.leaves(shard)
    sequence = sorted(range(len(leaves)), key=lambda k: -leaves[k].size)
    width = (1, *leaves[sequence[0]].shape)[-1]
    lines = [
        jnp.pad(leaves[k].reshape(-1), (0, -leaves[k].size % width)).reshape(-1, width)
        for k in sequence
    ]
    both, at, found = (copy_for_each(jnp.concatenate(lines), axis), 0, {})
    for k, line in zip(sequence, lines):
        slab = both[:, at : at + len(line)].reshape(len(both), -1)
        found[k] = slab[:, : leaves[k].size].reshape(-1, *leaves[k].shape)
        at += len(line)
    numbers = iter(range(len(leaves)))
    return jax.tree.map(lambda _: found[next(numbers)], shard)


def folded_in_pairs(pieces, combine):
    while len(jax.tree.leaves(pieces)[0]) > 1:
        pieces = jax.vmap(combine)(
            *(jax.tree.map(lambda part: part[side::2], pieces) for side in (0, 1))
        )
    return jax.tree.map(lambda part: part[0], pieces)


def carried_in(shard, axis, combine, identity):
    count, position = (lax.axis_size(axis), lax.axis_index(axis))
    passed = jnp.arange(count) < position

    def carried_kept(part, zero, own):
        part = jnp.where(
            passed.reshape(-1, *(1 for _ in own.shape)), part, jnp.asarray(zero, own.dtype)
        )
        return part

    pieces = gathered_once(shard, axis)
    return folded_in_pairs(jax.tree.map(carried_kept, pieces, identity, shard), combine)


def collected_alike(shard, axis):
    leaves, found = (jax.tree.leaves(shard), {})
    for initial, a in enumerate(leaves):
        if initial not in found:
            alike = [k for k, b in enumerate(leaves) if b.dtype == a.dtype]
            got = (
                gathered_once([leaves[k] for k in alike], axis)
                if len(alike) > 1
                else [copy_for_each(a, axis)]
            )
            for k, b in zip(alike, got):
                found[k] = b
    numbers = iter(range(len(leaves)))
    return jax.tree.map(lambda _: found[next(numbers)], shard)


def entering_2(shard, axis, combine, identity):
    count, position = (lax.axis_size(axis), lax.axis_index(axis))
    passed = jnp.arange(count) > position

    def entering_kept(part, zero, own):
        part = jnp.where(
            passed.reshape(-1, *(1 for _ in own.shape)), part, jnp.asarray(zero, own.dtype)
        )
        return part[::-1]

    pieces = collected_alike(shard, axis)
    return folded_in_pairs(jax.tree.map(entering_kept, pieces, identity, shard), combine)


def compose(earlier, later):
    return (later[0] * earlier[0], later[0] * earlier[1] + later[1])


def band_recurrence(factor, source, reverse_order):
    modes, rows, columns = factor.shape
    block = min(8, rows)
    groups = rows // block
    factor_blocks = factor.reshape(modes, groups, block, columns)
    source_blocks = source.reshape(modes, groups, block, columns)
    order = list(range(block))
    if reverse_order:
        order = order[::-1]
    running_scale = jnp.ones((modes, groups, columns), jnp.float32)
    running_shift = jnp.zeros((modes, groups, columns), jnp.float32)
    scale_rows = [None] * block
    shift_rows = [None] * block
    for position in order:
        step_factor = factor_blocks[:, :, position, :]
        running_scale = step_factor * running_scale
        running_shift = step_factor * running_shift + source_blocks[:, :, position, :]
        scale_rows[position] = running_scale
        shift_rows[position] = running_shift
    group_order = list(range(groups))
    if reverse_order:
        group_order = group_order[::-1]
    carry_scale = jnp.ones((modes, columns), jnp.float32)
    carry_shift = jnp.zeros((modes, columns), jnp.float32)
    enter_scale = [None] * groups
    enter_shift = [None] * groups
    for group in group_order:
        enter_scale[group] = carry_scale
        enter_shift[group] = carry_shift
        carry_scale, carry_shift = compose(
            (carry_scale, carry_shift), (running_scale[:, group, :], running_shift[:, group, :])
        )
    local_scale = jnp.stack(scale_rows, axis=2)
    local_shift = jnp.stack(shift_rows, axis=2)
    group_scale = jnp.stack(enter_scale, axis=1)[:, :, None, :]
    group_shift = jnp.stack(enter_shift, axis=1)[:, :, None, :]
    full_scale = (local_scale * group_scale).reshape(modes, rows, columns)
    full_shift = (local_shift + local_scale * group_shift).reshape(modes, rows, columns)
    return (full_scale, full_shift, (carry_scale, carry_shift))


def per_device(
    forcing, metric_lon, metric_lat, lon_weights, eigen_basis, lower_mult, pivot_inverse, upper_coef
):
    wrapped = padded(forcing, (("lon", 2),), 1, True)
    stacked = padded(forcing, (("lat", 1),), 1, False)
    source_term = (
        forcing
        + metric_lon * (wrapped[:, :, :-2] + wrapped[:, :, 2:])
        + metric_lat * (stacked[:, :-2, :] + stacked[:, 2:, :])
    )
    weighted = source_term * lon_weights
    spectral = jnp.einsum(
        "kji,im->kjm",
        lax.all_to_all(weighted, "lon", split_axis=0, concat_axis=2, tiled=True),
        eigen_basis,
        precision=lax.Precision.HIGHEST,
    )
    down_scale, down_shift, down_summary = band_recurrence(-lower_mult, spectral, False)
    identity = (jnp.ones_like(down_summary[0]), jnp.zeros_like(down_summary[1]))
    entering = carried_in(down_summary, "lat", compose, identity)[1]
    sweep = down_shift + down_scale * entering[:, None, :]
    up_factor = -(upper_coef * pivot_inverse)
    up_source = pivot_inverse * sweep
    up_scale, up_shift, up_summary = band_recurrence(up_factor, up_source, True)
    identity_up = (jnp.ones_like(up_summary[0]), jnp.zeros_like(up_summary[1]))
    arriving = entering_2(up_summary, "lat", compose, identity_up)[1]
    modal = up_shift + up_scale * arriving[:, None, :]
    on_grid = jnp.einsum("kjm,im->kji", modal, eigen_basis, precision=lax.Precision.HIGHEST)
    return lax.all_to_all(on_grid, "lon", split_axis=2, concat_axis=0, tiled=True)


def solution(mesh):
    placed = (
        P(None, "lat", "lon"),
        P("lat", "lon"),
        P("lat", "lon"),
        P("lon"),
        P(),
        P("lon", "lat", None),
        P("lon", "lat", None),
        P("lon", "lat", None),
    )
    return jax.shard_map(
        per_device, mesh=mesh, in_specs=placed, out_specs=P(None, "lat", "lon"), check_vma=False
    )
```

profile of v0, /device:TPU:1, one launch (start us, length us, event | category | flops | bytes accessed | tf_op | source)
XLA Modules:
  0.0 222.5 jit_solution(854617699514591773)
XLA Ops:
  0.0 1.0 fusion.109
  1.0 4.9 %collective-permute-start.2 = (f32[16,1,256]{2,1,0:T(1,128)S(1)}, f32[16,1,256]{2,1,0:T(1,128)S(1)}, u32[]{:S(2)}, u32[]{:S(2)}) collective-permute-start(f32[16,1,256]{2,1,0:T(1,128)S(1)} %get-tuple-element.92), channel_id=1, source_target_pairs={{0,8},{8,16},{16,24},{24,32},{32,40},{40,48},{48,56},{56,64},{64,7... | collective-permute-start | bytes 49160 | tf_op jit(solution)/shard_map/ppermute | solution.py:14
  5.9 1.9 collective-permute-start.3
  7.9 2.9 %fusion.108 = (f32[16,128,1]{2,1,0:T(8,128)}, f32[16,128,1]{2,1,0:T(8,128)S(1)}) fusion(f32[16,128,256]{2,1,0:T(8,128)} %param.8), kind=kLoop, calls=%fused_computation.380 | loop fusion | bytes 32768 | tf_op jit(solution)/shard_map/slice | solution.py:12
  10.7 1.7 copy.151
  12.5 2.8 %collective-permute-start = (f32[16,128,1]{1,0,2:T(8,128)S(1)}, f32[16,128,1]{1,0,2:T(8,128)S(1)}, u32[]{:S(2)}, u32[]{:S(2)}) collective-permute-start(f32[16,128,1]{1,0,2:T(8,128)S(1)} %copy.151), channel_id=1, source_target_pairs={{0,1},{1,2},{2,3},{3,4},{4,5},{5,6},{6,7},{7,0},{8,9},{9,10},{10,1... | collective-permute-start | bytes 24584 | tf_op jit(solution)/shard_map/ppermute | solution.py:14
  15.6 2.5 %collective-permute-start.1 = (f32[16,128,1]{1,0,2:T(8,128)S(1)}, f32[16,128,1]{1,0,2:T(8,128)S(1)}, u32[]{:S(2)}, u32[]{:S(2)}) collective-permute-start(f32[16,128,1]{1,0,2:T(8,128)S(1)} %copy.152), channel_id=1, source_target_pairs={{1,0},{2,1},{3,2},{4,3},{5,4},{6,5},{7,6},{0,7},{9,8},{10,9},{11,1... | collective-permute-start | bytes 24584 | tf_op jit(solution)/shard_map/ppermute | solution.py:15
  19.6 1.4 copy.101
  21.0 4.0 %fusion.7 = f32[16,128,256]{2,1,0:T(8,128)} fusion(f32[16,1,256]{2,1,0:T(1,128)S(1)} %collective-permute-done.3, f32[16,128,256]{2,1,0:T(8,128)S(1)} %copy-done.1, f32[16,1,256]{2,1,0:T(1,128)S(1)} %collective-permute-done.2, f32[16,128,1]{2,1,0:T(8,128)} %copy.101, f32[16,128,1]{2,1,0:T(8,128)S(1)} %copy.99, f32[256]{0:T(256)S(1)} %copy-done.22, ...), kind=kLoop, calls=%fused_computation.8 | loop fusion | flops 5767168 | bytes 4506624 | tf_op jit(solution)/shard_map/mul | solution.py:151
  25.0 6.3 %all-to-all-start = ((f32[16,128,256]{2,1,0:T(8,128)}), f32[16,128,256]{2,1,0:T(8,128)S(1)}, u32[]{:S(2)}, u32[]{:S(2)}) async-start(f32[16,128,256]{2,1,0:T(8,128)} %fusion.7), calls=%async_computation | async-start | bytes 4194304 | tf_op jit(solution)/shard_map/all_to_all | solution.py:154
  32.6 3.1 %negate_bitcast_fusion = f32[2,16,8,2048]{3,2,1,0:T(8,128)} fusion(f32[2,128,2048]{2,1,0:T(8,128)} %param.13), kind=kLoop, calls=%fused_computation.27 | loop fusion | flops 524288 | bytes 4194304 | tf_op jit(solution)/shard_map/reshape | solution.py:104
  35.7 24.1 %all-to-all-done = f32[16,128,256]{2,1,0:T(8,128)S(1)} async-done(((f32[16,128,256]{2,1,0:T(8,128)}), f32[16,128,256]{2,1,0:T(8,128)S(1)}, u32[]{:S(2)}, u32[]{:S(2)}) %all-to-all-start) | async-done | bytes 2097184 | tf_op jit(solution)/shard_map/all_to_all | solution.py:154
  59.8 2.5 %copy.532 = f32[8,2,128,256]{3,0,2,1:T(8,128)} copy(f32[8,2,128,256]{3,2,1,0:T(8,128)S(1)} %bitcast.627) | data formatting | bytes 4194304 | tf_op jit(solution)/shard_map/all_to_all | solution.py:154
  62.3 1.7 dot_general.8
  64.0 17.1 %fusion = f32[2,16,8,2048]{3,2,1,0:T(8,128)S(1)} fusion(f32[2,16,8,2048]{3,2,1,0:T(8,128)S(1)} %dot_general.8, f32[2048,2048]{1,0:T(8,128)} %param.12), kind=kOutput, calls=%fused_computation | convolution fusion | flops 12884901888 | bytes 20971520 | tf_op jit(solution)/shard_map/kji,im->kjm/dot_general | solution.py:152
  81.2 3.2 %fusion.107 = (f32[2,16,1,2048]{3,2,1,0:T(1,128)S(1)}, f32[2,16,1,2048]{3,2,1,0:T(1,128)S(1)}, f32[2,16,1,2048]{3,2,1,0:T(1,128)S(1)}, f32[2,16,1,2048]{3,2,1,0:...) fusion(f32[2,16,8,2048]{3,2,1,0:T(8,128)S(1)} %fusion, ...), kind=kLoop, calls=%fused_computation.379 | loop fusion | bytes 8388608 | tf_op jit(solution)/shard_map/slice | solution.py:116
  84.5 1.2 constant_dynamic-update-slice_fusion.6
  85.7 2.2 fusion.33
  90.2 0.9 broadcast_in_dim.48
  91.1 6.8 %all-to-all-start.1 = ((f32[16,4,2048]{2,1,0:T(4,128)}), f32[16,4,2048]{2,1,0:T(4,128)}, u32[]{:S(2)}, u32[]{:S(2)}) async-start(f32[16,4,2048]{2,1,0:T(4,128)} %broadcast_in_dim.48), calls=%async_computation.1 | async-start | bytes 1048576 | tf_op jit(solution)/shard_map/all_to_all | solution.py:22
  97.9 1.6 constant_dynamic-update-slice_fusion.5
  99.5 1.5 constant_dynamic-update-slice_fusion.4
  101.0 1.9 constant_dynamic-update-slice_fusion.3
  102.9 1.3 constant_dynamic-update-slice_fusion.2
  104.3 1.7 constant_dynamic-update-slice_fusion.1
  106.0 1.3 constant_dynamic-update-slice_fusion
  107.4 1.6 fusion.46
  109.0 4.1 %multiply_add_fusion.1 = (f32[8,4,8,2048]{3,0,1,2:T(8,128)S(1)}, f32[8,4,8,2048]{3,0,1,2:T(8,128)}) fusion(f32[8,4,8,2048]{3,0,1,2:T(8,128)} %bitcast.632, f32[8,4,8,2048]{3,0,1,2:T(8,128)} %bitcast.633, f32[8,4,2048]{2,0,1:T(8,128)S(1)} %bitcast.635, f32[8,4,2048]{2,0,1:T(8,128)S(1)} %bitcast.634), kind=kLoop, calls=%fused_computation.26 | loop fusion | flops 1572864 | bytes 8912896 | tf_op jit(solution)/shard_map/add | solution.py:137
  113.1 1.7 slice_select_fusion.3
  115.1 4.9 %fusion.16 = (f32[2,16,8,2048]{3,2,1,0:T(8,128)S(1)}, f32[2,16,8,2048]{3,2,1,0:T(8,128)S(1)}) fusion(f32[2,128,2048]{2,1,0:T(8,128)} %param.14, f32[2,16,8,2048]{3,0,1,2:T(2,128)S(1)} %bitcast.626, f32[2,16,8,2048]{3,0,1,2:T(2,128)S(1)} %bitcast.625, f32[2,2048]{1,0:T(2,128)S(1)} %fusion.49, f32[2,128,2048]{2,1,0:T(8,128)} %param.15), kind=kLoop, calls=%fused_computation.21 | loop fusion | flops 2621440 | bytes 12599296 | tf_op jit(solution)/shard_map/reshape | solution.py:105
  120.0 1.4 fusion.106
  121.5 1.7 fusion.111
  123.1 2.4 %bitcast_add_fusion.1 = (f32[2,16,2048]{2,0,1:T(2,128)S(1)}, f32[2,16,2048]{2,0,1:T(2,128)S(1)}) fusion(f32[2,16,1,2048]{3,2,1,0:T(1,128)S(1)} %get-tuple-element.75, f32[2,16,1,2048]{3,2,1,0:T(1,128)S(1)} %get-tuple-element.69, f32[2,16,1,2048]{3,2,1,0:T(1,128)S(1)} %get-tuple-element.70, f32[2,16,1,2048]{3,2,1,0:T(1,128)S(1)} %get-tuple-element.71, ...), kind=kLoop, calls=%fused_computation.37 | loop fusion | flops 1507328 | bytes 4718592 | tf_op jit(solution)/shard_map/add | solution.py:116
  125.9 3.7 %add_dynamic-update-slice_fusion = (f32[2,16,8,2048]{3,0,1,2:T(2,128)}, f32[2,16,1,2048]{3,0,1,2:T(2,128)}, f32[2,16,1,2048]{3,0,1,2:T(2,128)S(1)}, f32[2,16,1,2...) fusion(f32[2,16,1,2048]{3,2,1,0:T(1,128)S(1)} %get-tuple-elemen, ...), kind=kLoop, calls=%fused_computation.85 | loop fusion | flops 1507326 | bytes 6029312
  131.5 0.9 broadcast_in_dim.52
  132.4 5.7 %all-to-all-start.2 = ((f32[16,4,2048]{2,1,0:T(4,128)}), f32[16,4,2048]{2,1,0:T(4,128)}, u32[]{:S(2)}, u32[]{:S(2)}) async-start(f32[16,4,2048]{2,1,0:T(4,128)} %broadcast_in_dim.52), calls=%async_computation.2 | async-start | bytes 1048576 | tf_op jit(solution)/shard_map/all_to_all | solution.py:22
  138.1 2.3 %constant_dynamic-update-slice_fusion.52 = (f32[2,16,8,2048]{3,0,1,2:T(2,128)}, f32[2,16,8,2048]{3,0,1,2:T(2,128)}) fusion(f32[2,16,8,2048]{3,0,1,2:T(2,128)} %get-tuple-element.13, f32[2,16,1,2048]{3,2,1,0:T(1,128)S(1)} %get-tuple-element.69, f32[2,16,1,2048]{3,0,1,2:T(2,128)} %get-tuple-element.14, f32[2,16,1,2048]{3,2,1,0:T(1,128)S(1)} %get-tuple-element.107, ...), kind=kLoop, calls=%fused_computation.153 | loop fusion | flops 196608 | bytes 1572864
  140.4 1.7 constant_dynamic-update-slice_fusion.51
  142.8 1.3 constant_dynamic-update-slice_fusion.50
  145.6 1.5 constant_dynamic-update-slice_fusion.48
  147.8 1.4 constant_dynamic-update-slice_fusion.46
  149.2 0.9 constant_dynamic-update-slice_fusion.53
  150.1 4.2 %multiply_add_fusion = (f32[8,4,8,2048]{3,0,1,2:T(8,128)S(1)}, f32[8,4,8,2048]{3,0,1,2:T(8,128)}) fusion(f32[8,4,8,2048]{3,0,1,2:T(8,128)} %bitcast.630, f32[8,4,8,2048]{3,0,1,2:T(8,128)} %bitcast.631, f32[8,4,2048]{2,0,1:T(8,128)S(1)} %bitcast.636, f32[8,4,2048]{2,0,1:T(8,128)S(1)} %bitcast.637), kind=kLoop, calls=%fused_computation.25 | loop fusion | flops 1572864 | bytes 8912896 | tf_op jit(solution)/shard_map/add | solution.py:137
  154.3 1.7 slice_select_fusion.1
  156.3 27.4 %fusion.2 = f32[2,128,2048]{2,1,0:T(8,128)} fusion(f32[2048,2048]{1,0:T(8,128)} %param.12, f32[2,16,8,2048]{3,0,1,2:T(2,128)S(1)} %bitcast.624, f32[2,16,8,2048]{3,0,1,2:T(2,128)S(1)} %bitcast.623, f32[2,2048]{1,0:T(2,128)S(1)} %fusion.47), kind=kOutput, calls=%fused_computation.2 | convolution fusion | flops 12885950464 | bytes 23085056 | tf_op jit(solution)/shard_map/kjm,im->kji/dot_general | solution.py:168
  183.7 2.8 %copy.146 = f32[2,128,2048]{1,0,2:T(2,128)S(1)} copy(f32[2,128,2048]{2,1,0:T(8,128)} %fusion.2) | data formatting | bytes 4194304 | tf_op jit(solution)/shard_map/kjm,im->kji/dot_general | solution.py:168
  186.6 31.5 %all_to_all.43 = f32[2,128,2048]{1,0,2:T(2,128)} all-to-all(f32[2,128,2048]{1,0,2:T(2,128)S(1)} %copy.146), channel_id=1, replica_groups=mesh['lat'=16,'lon'=8] {'lon'}, dimensions={2} | all-to-all | bytes 4194304 | tf_op jit(solution)/shard_map/all_to_all | solution.py:169
  218.1 4.1 %copy.147 = f32[8,2,128,256]{3,2,1,0:T(8,128)} copy(f32[8,2,128,256]{2,1,3,0:T(2,128)} %bitcast.629) | data formatting | bytes 4194304 | tf_op jit(solution)/shard_map/all_to_all | solution.py:169
  (136 shorter events, 11.0 us)
Async XLA Ops:
  1.0 20.0 %collective-permute-start.2 = (f32[16,1,256]{2,1,0:T(1,128)S(1)}, f32[16,1,256]{2,1,0:T(1,128)S(1)}, u32[]{:S(2)}, u32[]{:S(2)}) collective-permute-start(f32[16,1,256]{2,1,0:T(1,128)S(1)} %get-tuple-element.92), channel_id=1, source_target_pairs={{0,8},{8,16},{16,24},{24,32},{32,40},{40,48},{48,56},{56,64},{64,7... | collective-permute-start | bytes 49160 | tf_op jit(solution)/shard_map/ppermute | solution.py:14
  5.9 15.0 %collective-permute-start.3 = (f32[16,1,256]{2,1,0:T(1,128)S(1)}, f32[16,1,256]{2,1,0:T(1,128)S(1)}, u32[]{:S(2)}, u32[]{:S(2)}) collective-permute-start(f32[16,1,256]{2,1,0:T(1,128)S(1)} %get-tuple-element.93), channel_id=1, source_target_pairs={{8,0},{16,8},{24,16},{32,24},{40,32},{48,40},{56,48},{64,56},{72,6... | collective-permute-start | bytes 49160 | tf_op jit(solution)/shard_map/ppermute | solution.py:15
  10.7 10.2 %copy-start.1 = (f32[16,128,256]{2,1,0:T(8,128)S(1)}, f32[16,128,256]{2,1,0:T(8,128)}, u32[]{:S(2)}) copy-start(f32[16,128,256]{2,1,0:T(8,128)} %param.8) | copy-start | bytes 6291460
  10.7 10.2 %copy-start.20 = (f32[128,256]{1,0:T(8,128)S(1)}, f32[128,256]{1,0:T(8,128)}, u32[]{:S(2)}) copy-start(f32[128,256]{1,0:T(8,128)} %param.10) | copy-start | bytes 393220
  10.7 10.2 %copy-start.21 = (f32[128,256]{1,0:T(8,128)S(1)}, f32[128,256]{1,0:T(8,128)}, u32[]{:S(2)}) copy-start(f32[128,256]{1,0:T(8,128)} %param.9) | copy-start | bytes 393220
  10.7 10.3 %copy-start.22 = (f32[256]{0:T(256)S(1)}, f32[256]{0:T(256)}, u32[]{:S(2)}) copy-start(f32[256]{0:T(256)} %param.11) | copy-start | bytes 3076
  12.5 6.3 %collective-permute-start = (f32[16,128,1]{1,0,2:T(8,128)S(1)}, f32[16,128,1]{1,0,2:T(8,128)S(1)}, u32[]{:S(2)}, u32[]{:S(2)}) collective-permute-start(f32[16,128,1]{1,0,2:T(8,128)S(1)} %copy.151), channel_id=1, source_target_pairs={{0,1},{1,2},{2,3},{3,4},{4,5},{5,6},{6,7},{7,0},{8,9},{9,10},{10,1... | collective-permute-start | bytes 24584 | tf_op jit(solution)/shard_map/ppermute | solution.py:14
  15.6 4.0 %collective-permute-start.1 = (f32[16,128,1]{1,0,2:T(8,128)S(1)}, f32[16,128,1]{1,0,2:T(8,128)S(1)}, u32[]{:S(2)}, u32[]{:S(2)}) collective-permute-start(f32[16,128,1]{1,0,2:T(8,128)S(1)} %copy.152), channel_id=1, source_target_pairs={{1,0},{2,1},{3,2},{4,3},{5,4},{6,5},{7,6},{0,7},{9,8},{10,9},{11,1... | collective-permute-start | bytes 24584 | tf_op jit(solution)/shard_map/ppermute | solution.py:15
  25.0 34.8 %all-to-all-start = ((f32[16,128,256]{2,1,0:T(8,128)}), f32[16,128,256]{2,1,0:T(8,128)S(1)}, u32[]{:S(2)}, u32[]{:S(2)}) async-start(f32[16,128,256]{2,1,0:T(8,128)} %fusion.7), calls=%async_computation | async-start | bytes 4194304 | tf_op jit(solution)/shard_map/all_to_all | solution.py:154
  64.0 17.2 %copy-start.3 = (f32[2,16,8,2048]{3,2,1,0:T(8,128)S(1)}, f32[2,16,8,2048]{3,2,1,0:T(8,128)}, u32[]{:S(2)}) copy-start(f32[2,16,8,2048]{3,2,1,0:T(8,128)} %negate_bitcast_fusion) | copy-start | bytes 6291460
  84.5 3.4 %copy-start.4 = (f32[2,16,1,2048]{3,2,1,0:T(1,128)}, f32[2,16,1,2048]{3,2,1,0:T(1,128)S(1)}, u32[]{:S(2)}) copy-start(f32[2,16,1,2048]{3,2,1,0:T(1,128)S(1)} %get-tuple-element.189) | copy-start | bytes 786436
  84.5 3.4 %copy-start.6 = (f32[2,16,1,2048]{3,2,1,0:T(1,128)}, f32[2,16,1,2048]{3,2,1,0:T(1,128)S(1)}, u32[]{:S(2)}) copy-start(f32[2,16,1,2048]{3,2,1,0:T(1,128)S(1)} %get-tuple-element.85) | copy-start | bytes 786436
  84.5 3.4 %copy-start.8 = (f32[2,16,1,2048]{3,2,1,0:T(1,128)}, f32[2,16,1,2048]{3,2,1,0:T(1,128)S(1)}, u32[]{:S(2)}) copy-start(f32[2,16,1,2048]{3,2,1,0:T(1,128)S(1)} %get-tuple-element.186) | copy-start | bytes 786436
  85.7 2.8 %copy-start.13 = (f32[2,16,2048]{2,0,1:T(2,128)S(1)}, f32[2,16,2048]{2,0,1:T(2,128)}, u32[]{:S(2)}) copy-start(f32[2,16,2048]{2,0,1:T(2,128)} %constant_dynamic-update-slice_fusion.29) | copy-start | bytes 786436
  87.9 1.2 copy-start.10
  89.1 1.1 copy-start.14
  89.4 0.7 copy-start.11
  91.1 22.0 %all-to-all-start.1 = ((f32[16,4,2048]{2,1,0:T(4,128)}), f32[16,4,2048]{2,1,0:T(4,128)}, u32[]{:S(2)}, u32[]{:S(2)}) async-start(f32[16,4,2048]{2,1,0:T(4,128)} %broadcast_in_dim.48), calls=%async_computation.1 | async-start | bytes 1048576 | tf_op jit(solution)/shard_map/all_to_all | solution.py:22
  97.9 3.2 %copy-start.7 = (f32[2,16,1,2048]{3,2,1,0:T(1,128)S(1)}, f32[2,16,1,2048]{3,2,1,0:T(1,128)}, u32[]{:S(2)}) copy-start(f32[2,16,1,2048]{3,2,1,0:T(1,128)} %copy-done.6) | copy-start | bytes 786436
  97.9 3.1 %copy-start.9 = (f32[2,16,1,2048]{3,2,1,0:T(1,128)S(1)}, f32[2,16,1,2048]{3,2,1,0:T(1,128)}, u32[]{:S(2)}) copy-start(f32[2,16,1,2048]{3,2,1,0:T(1,128)} %copy-done.8) | copy-start | bytes 786436
  104.3 3.1 %copy-start.5 = (f32[2,16,1,2048]{3,2,1,0:T(1,128)S(1)}, f32[2,16,1,2048]{3,2,1,0:T(1,128)}, u32[]{:S(2)}) copy-start(f32[2,16,1,2048]{3,2,1,0:T(1,128)} %copy-done.4) | copy-start | bytes 786436
  106.0 2.9 %copy-start.12 = (f32[2,16,2048]{2,0,1:T(2,128)S(1)}, f32[2,16,2048]{2,0,1:T(2,128)}, u32[]{:S(2)}) copy-start(f32[2,16,2048]{2,0,1:T(2,128)} %copy-done.11) | copy-start | bytes 786436
  106.0 2.9 %copy-start.15 = (f32[2,16,2048]{2,0,1:T(2,128)S(1)}, f32[2,16,2048]{2,0,1:T(2,128)}, u32[]{:S(2)}) copy-start(f32[2,16,2048]{2,0,1:T(2,128)} %copy-done.14) | copy-start | bytes 786436
  113.1 2.0 copy-start.2
  130.1 0.7 copy-start.16
  130.8 0.7 copy-start.18
  132.4 21.9 %all-to-all-start.2 = ((f32[16,4,2048]{2,1,0:T(4,128)}), f32[16,4,2048]{2,1,0:T(4,128)}, u32[]{:S(2)}, u32[]{:S(2)}) async-start(f32[16,4,2048]{2,1,0:T(4,128)} %broadcast_in_dim.52), calls=%async_computation.2 | async-start | bytes 1048576 | tf_op jit(solution)/shard_map/all_to_all | solution.py:22
  145.6 4.5 %copy-start.17 = (f32[2,16,2048]{2,0,1:T(2,128)S(1)}, f32[2,16,2048]{2,0,1:T(2,128)}, u32[]{:S(2)}) copy-start(f32[2,16,2048]{2,0,1:T(2,128)} %copy-done.16) | copy-start | bytes 786436
  145.6 4.5 %copy-start.19 = (f32[2,16,2048]{2,0,1:T(2,128)S(1)}, f32[2,16,2048]{2,0,1:T(2,128)}, u32[]{:S(2)}) copy-start(f32[2,16,2048]{2,0,1:T(2,128)} %copy-done.18) | copy-start | bytes 786436
  154.3 2.1 copy-start
where the time goes:
time: 226 us; the launch traced here: 222 us
  other arithmetic  53.2 us (24%)
  matrix products  44.6 us (20%)
  local copies, waits for them, and re-layouts  36.1 us (16%)
  blocking collectives  31.5 us (14%)
  starting transfers between devices  31 us (14%)
  waiting for transfers between devices  25.3 us (11%)
    all_to_all x1, blocking collectives, per_device(): lax.all_to_all(on_grid, 'lon', split_axis=2, concat_axis=0, tiled=True)  31.5 us
    dot_general x1, matrix products, per_device(): jnp.einsum('kjm,im->kji', modal, eigen_basis, precision=lax.Precision.HIG...  27.4 us
    all_to_all x1, waiting for transfers between devices, per_device(): lax.all_to_all(weighted, 'lon', split_axis=0, concat_axis=2, tiled=True)  24.1 us
    unnamed x49, other arithmetic  20.7 us
    dot_general x1, matrix products, per_device(): jnp.einsum('kji,im->kjm', lax.all_to_all(weighted, 'lon', split_axis=0, c...  17.1 us
    all_to_all x2, starting transfers between devices, copy_for_each(): lax.all_to_all(jnp.broadcast_to(shard[None], (count, *shard.shape)), axis...  12.5 us
    unnamed x69, local copies, waits for them, and re-layouts  10.1 us
    add x2, other arithmetic, band_recurrence(): local_shift + local_scale * group_shift  8.31 us
  transfers between devices with their start and end apart: 7, of which 3 were waited for; matrix products, arithmetic and copies ran while one was open for 19% of the time, Pallas kernels for 0%

commit v1 on v0

--- a/solution.py
+++ b/solution.py
@@ -2,6 +2,7 @@
 import jax.numpy as jnp
 from jax import lax
 from jax.sharding import PartitionSpec as P
+from jax.lax import all_to_all, axis_size
 
 
 def padded(shard, sides, width, wrap):
@@ -166,7 +167,9 @@
     arriving = entering_2(up_summary, "lat", compose, identity_up)[1]
     modal = up_shift + up_scale * arriving[:, None, :]
     on_grid = jnp.einsum("kjm,im->kji", modal, eigen_basis, precision=lax.Precision.HIGHEST)
-    return lax.all_to_all(on_grid, "lon", split_axis=2, concat_axis=0, tiled=True)
+    return jnp.concatenate(
+        all_to_all(jnp.stack(jnp.split(on_grid, axis_size("lon"), axis=2)), "lon", 0, 0), axis=0
+    )
 
 
 def solution(mesh):

time: 226 us -> 219 us (0.969)
  local copies, waits for them, and re-layouts: 36.1 us -> 30.6 us
    all_to_all x1 -> x0, local copies, waits for them, and re-layouts: 4.11 us -> none  [per_device(): lax.all_to_all(on_grid, 'lon', split_axis=2, concat_axis=0, tiled=True)]
    dot_general x1 -> x0, local copies, waits for them, and re-layouts: 2.85 us -> none  [per_device(): jnp.einsum('kjm,im->kji', modal, eigen_basis, precision=lax.Precision.HIG...]
    unnamed x69 -> x77, local copies, waits for them, and re-layouts: 10.1 us -> 11.5 us
  transfers between devices with their start and end apart: 7 -> 7, of which waited for: 3 -> 3; matrix products, arithmetic and copies ran while one was open for 19% -> 20% of each run, Pallas kernels for 0% -> 0%
where the time goes in v1:
time: 219 us; the launch traced here: 216 us
  other arithmetic  53.2 us (24%)
  matrix products  43.8 us (20%)
  starting transfers between devices  31 us (14%)
  blocking collectives  30.9 us (14%)
  local copies, waits for them, and re-layouts  30.6 us (14%)
  waiting for transfers between devices  25.3 us (12%)
    all_to_all x1, blocking collectives, per_device(): all_to_all(jnp.stack(jnp.split(on_grid, axis_size('lon'), axis=2)), 'lon'...  30.9 us
    dot_general x1, matrix products, per_device(): jnp.einsum('kjm,im->kji', modal, eigen_basis, precision=lax.Precision.HIG...  26.6 us
    all_to_all x1, waiting for transfers between devices, per_device(): lax.all_to_all(weighted, 'lon', split_axis=0, concat_axis=2, tiled=True)  24.1 us
    unnamed x49, other arithmetic  20.7 us
    dot_general x1, matrix products, per_device(): jnp.einsum('kji,im->kjm', lax.all_to_all(weighted, 'lon', split_axis=0, c...  17.1 us
    all_to_all x2, starting transfers between devices, copy_for_each(): lax.all_to_all(jnp.broadcast_to(shard[None], (count, *shard.shape)), axis...  12.5 us
    unnamed x77, local copies, waits for them, and re-layouts  11.5 us
    add x2, other arithmetic, band_recurrence(): local_shift + local_scale * group_shift  8.31 us
  transfers between devices with their start and end apart: 7, of which 3 were waited for; matrix products, arithmetic and copies ran while one was open for 20% of the time, Pallas kernels for 0%

profile of v1, /device:TPU:1, one launch (start us, length us, event | category | flops | bytes accessed | tf_op | source)
XLA Modules:
  0.0 215.6 jit_solution(16266097610069696577)
XLA Ops:
  0.0 1.0 fusion.117
  1.0 4.9 %collective-permute-start.2 = (f32[16,1,256]{2,1,0:T(1,128)S(1)}, f32[16,1,256]{2,1,0:T(1,128)S(1)}, u32[]{:S(2)}, u32[]{:S(2)}) collective-permute-start(f32[16,1,256]{2,1,0:T(1,128)S(1)} %get-tuple-element.92), channel_id=1, source_target_pairs={{0,8},{8,16},{16,24},{24,32},{32,40},{40,48},{48,56},{56,64},{64,7... | collective-permute-start | bytes 49160 | tf_op jit(solution)/shard_map/ppermute | solution.py:15
  5.9 1.9 collective-permute-start.3
  7.9 2.9 %fusion.116 = (f32[16,128,1]{2,1,0:T(8,128)}, f32[16,128,1]{2,1,0:T(8,128)S(1)}) fusion(f32[16,128,256]{2,1,0:T(8,128)} %param.8), kind=kLoop, calls=%fused_computation.396 | loop fusion | bytes 32768 | tf_op jit(solution)/shard_map/slice | solution.py:13
  10.7 1.7 copy.147
  12.5 2.8 %collective-permute-start = (f32[16,128,1]{1,0,2:T(8,128)S(1)}, f32[16,128,1]{1,0,2:T(8,128)S(1)}, u32[]{:S(2)}, u32[]{:S(2)}) collective-permute-start(f32[16,128,1]{1,0,2:T(8,128)S(1)} %copy.147), channel_id=1, source_target_pairs={{0,1},{1,2},{2,3},{3,4},{4,5},{5,6},{6,7},{7,0},{8,9},{9,10},{10,1... | collective-permute-start | bytes 24584 | tf_op jit(solution)/shard_map/ppermute | solution.py:15
  15.6 2.5 %collective-permute-start.1 = (f32[16,128,1]{1,0,2:T(8,128)S(1)}, f32[16,128,1]{1,0,2:T(8,128)S(1)}, u32[]{:S(2)}, u32[]{:S(2)}) collective-permute-start(f32[16,128,1]{1,0,2:T(8,128)S(1)} %copy.148), channel_id=1, source_target_pairs={{1,0},{2,1},{3,2},{4,3},{5,4},{6,5},{7,6},{0,7},{9,8},{10,9},{11,1... | collective-permute-start | bytes 24584 | tf_op jit(solution)/shard_map/ppermute | solution.py:16
  19.6 1.4 copy.99
  21.0 4.0 %fusion.7 = f32[16,128,256]{2,1,0:T(8,128)} fusion(f32[16,1,256]{2,1,0:T(1,128)S(1)} %collective-permute-done.3, f32[16,128,256]{2,1,0:T(8,128)S(1)} %copy-done.1, f32[16,1,256]{2,1,0:T(1,128)S(1)} %collective-permute-done.2, f32[16,128,1]{2,1,0:T(8,128)} %copy.99, f32[16,128,1]{2,1,0:T(8,128)S(1)} %copy.97, f32[256]{0:T(256)S(1)} %copy-done.22, ...), kind=kLoop, calls=%fused_computation.8 | loop fusion | flops 5767168 | bytes 4506624 | tf_op jit(solution)/shard_map/mul | solution.py:152
  25.0 6.3 %all-to-all-start = ((f32[16,128,256]{2,1,0:T(8,128)}), f32[16,128,256]{2,1,0:T(8,128)S(1)}, u32[]{:S(2)}, u32[]{:S(2)}) async-start(f32[16,128,256]{2,1,0:T(8,128)} %fusion.7), calls=%async_computation | async-start | bytes 4194304 | tf_op jit(solution)/shard_map/all_to_all | solution.py:155
  32.6 3.1 %negate_bitcast_fusion = f32[2,16,8,2048]{3,2,1,0:T(8,128)} fusion(f32[2,128,2048]{2,1,0:T(8,128)} %param.13), kind=kLoop, calls=%fused_computation.27 | loop fusion | flops 524288 | bytes 4194304 | tf_op jit(solution)/shard_map/reshape | solution.py:105
  35.7 24.1 %all-to-all-done = f32[16,128,256]{2,1,0:T(8,128)S(1)} async-done(((f32[16,128,256]{2,1,0:T(8,128)}), f32[16,128,256]{2,1,0:T(8,128)S(1)}, u32[]{:S(2)}, u32[]{:S(2)}) %all-to-all-start) | async-done | bytes 2097184 | tf_op jit(solution)/shard_map/all_to_all | solution.py:155
  59.8 2.5 %copy.528 = f32[8,2,128,256]{3,0,2,1:T(8,128)} copy(f32[8,2,128,256]{3,2,1,0:T(8,128)S(1)} %bitcast.656) | data formatting | bytes 4194304 | tf_op jit(solution)/shard_map/all_to_all | solution.py:155
  62.3 1.7 dot_general.8
  64.0 17.1 %fusion = f32[2,16,8,2048]{3,2,1,0:T(8,128)S(1)} fusion(f32[2,16,8,2048]{3,2,1,0:T(8,128)S(1)} %dot_general.8, f32[2048,2048]{1,0:T(8,128)} %param.12), kind=kOutput, calls=%fused_computation | convolution fusion | flops 12884901888 | bytes 20971520 | tf_op jit(solution)/shard_map/kji,im->kjm/dot_general | solution.py:153
  81.2 3.2 %fusion.115 = (f32[2,16,1,2048]{3,2,1,0:T(1,128)S(1)}, f32[2,16,1,2048]{3,2,1,0:T(1,128)S(1)}, f32[2,16,1,2048]{3,2,1,0:T(1,128)S(1)}, f32[2,16,1,2048]{3,2,1,0:...) fusion(f32[2,16,8,2048]{3,2,1,0:T(8,128)S(1)} %fusion, ...), kind=kLoop, calls=%fused_computation.395 | loop fusion | bytes 8388608 | tf_op jit(solution)/shard_map/slice | solution.py:117
  84.5 1.2 constant_dynamic-update-slice_fusion.6
  85.7 2.2 %fusion.41 = (f32[2,16,2048]{2,0,1:T(2,128)S(1)}, f32[2,16,2048]{2,0,1:T(2,128)S(1)}) fusion(f32[2,16,1,2048]{3,2,1,0:T(1,128)S(1)} %get-tuple-element.89, f32[2,16,1,2048]{3,2,1,0:T(1,128)S(1)} %get-tuple-element.83, f32[2,16,1,2048]{3,2,1,0:T(1,128)S(1)} %get-tuple-element.84, f32[2,16,1,2048]{3,2,1,0:T(1,128)S(1)} %get-tuple-element.85, ...), kind=kLoop, calls=%fused_computation.77 | loop fusion | flops 1441792 | bytes 4456448 | tf_op jit(solution)/shard_map/mul | solution.py:117
  90.2 0.9 broadcast_in_dim.48
  91.1 6.8 %all-to-all-start.1 = ((f32[16,4,2048]{2,1,0:T(4,128)}), f32[16,4,2048]{2,1,0:T(4,128)}, u32[]{:S(2)}, u32[]{:S(2)}) async-start(f32[16,4,2048]{2,1,0:T(4,128)} %broadcast_in_dim.48), calls=%async_computation.1 | async-start | bytes 1048576 | tf_op jit(solution)/shard_map/all_to_all | solution.py:23
  97.9 1.6 constant_dynamic-update-slice_fusion.5
  99.5 1.5 constant_dynamic-update-slice_fusion.4
  101.0 1.9 constant_dynamic-update-slice_fusion.3
  102.9 1.3 constant_dynamic-update-slice_fusion.2
  104.3 1.7 constant_dynamic-update-slice_fusion.1
  106.0 1.3 constant_dynamic-update-slice_fusion
  107.4 1.6 fusion.54
  109.0 4.1 %multiply_add_fusion.1 = (f32[8,4,8,2048]{3,0,1,2:T(8,128)S(1)}, f32[8,4,8,2048]{3,0,1,2:T(8,128)}) fusion(f32[8,4,8,2048]{3,0,1,2:T(8,128)} %bitcast.661, f32[8,4,8,2048]{3,0,1,2:T(8,128)} %bitcast.662, f32[8,4,2048]{2,0,1:T(8,128)S(1)} %bitcast.664, f32[8,4,2048]{2,0,1:T(8,128)S(1)} %bitcast.663), kind=kLoop, calls=%fused_computation.26 | loop fusion | flops 1572864 | bytes 8912896 | tf_op jit(solution)/shard_map/add | solution.py:138
  113.1 1.7 slice_select_fusion.3
  115.1 4.9 %fusion.16 = (f32[2,16,8,2048]{3,2,1,0:T(8,128)S(1)}, f32[2,16,8,2048]{3,2,1,0:T(8,128)S(1)}) fusion(f32[2,128,2048]{2,1,0:T(8,128)} %param.14, f32[2,16,8,2048]{3,0,1,2:T(2,128)S(1)} %bitcast.655, f32[2,16,8,2048]{3,0,1,2:T(2,128)S(1)} %bitcast.654, f32[2,2048]{1,0:T(2,128)S(1)} %fusion.57, f32[2,128,2048]{2,1,0:T(8,128)} %param.15), kind=kLoop, calls=%fused_computation.21 | loop fusion | flops 2621440 | bytes 12599296 | tf_op jit(solution)/shard_map/reshape | solution.py:106
  120.0 1.4 fusion.114
  121.5 1.7 fusion.119
  123.1 2.4 %bitcast_add_fusion.1 = (f32[2,16,2048]{2,0,1:T(2,128)S(1)}, f32[2,16,2048]{2,0,1:T(2,128)S(1)}) fusion(f32[2,16,1,2048]{3,2,1,0:T(1,128)S(1)} %get-tuple-element.75, f32[2,16,1,2048]{3,2,1,0:T(1,128)S(1)} %get-tuple-element.69, f32[2,16,1,2048]{3,2,1,0:T(1,128)S(1)} %get-tuple-element.70, f32[2,16,1,2048]{3,2,1,0:T(1,128)S(1)} %get-tuple-element.71, ...), kind=kLoop, calls=%fused_computation.53 | loop fusion | flops 1507328 | bytes 4718592 | tf_op jit(solution)/shard_map/add | solution.py:117
  125.9 3.7 %add_dynamic-update-slice_fusion = (f32[2,16,8,2048]{3,0,1,2:T(2,128)}, f32[2,16,1,2048]{3,0,1,2:T(2,128)}, f32[2,16,1,2048]{3,0,1,2:T(2,128)S(1)}, f32[2,16,1,2...) fusion(f32[2,16,1,2048]{3,2,1,0:T(1,128)S(1)} %get-tuple-elemen, ...), kind=kLoop, calls=%fused_computation.101 | loop fusion | flops 1507326 | bytes 6029312
  131.5 0.9 broadcast_in_dim.52
  132.4 5.7 %all-to-all-start.2 = ((f32[16,4,2048]{2,1,0:T(4,128)}), f32[16,4,2048]{2,1,0:T(4,128)}, u32[]{:S(2)}, u32[]{:S(2)}) async-start(f32[16,4,2048]{2,1,0:T(4,128)} %broadcast_in_dim.52), calls=%async_computation.2 | async-start | bytes 1048576 | tf_op jit(solution)/shard_map/all_to_all | solution.py:23
  138.1 2.3 %constant_dynamic-update-slice_fusion.52 = (f32[2,16,8,2048]{3,0,1,2:T(2,128)}, f32[2,16,8,2048]{3,0,1,2:T(2,128)}) fusion(f32[2,16,8,2048]{3,0,1,2:T(2,128)} %get-tuple-element.13, f32[2,16,1,2048]{3,2,1,0:T(1,128)S(1)} %get-tuple-element.69, f32[2,16,1,2048]{3,0,1,2:T(2,128)} %get-tuple-element.14, f32[2,16,1,2048]{3,2,1,0:T(1,128)S(1)} %get-tuple-element.107, ...), kind=kLoop, calls=%fused_computation.169 | loop fusion | flops 196608 | bytes 1572864
  140.4 1.7 constant_dynamic-update-slice_fusion.51
  142.8 1.3 constant_dynamic-update-slice_fusion.50
  144.1 0.7 constant_dynamic-update-slice_fusion.49
  145.6 1.5 constant_dynamic-update-slice_fusion.48
  147.8 1.4 constant_dynamic-update-slice_fusion.46
  149.2 0.9 constant_dynamic-update-slice_fusion.53
  150.1 4.2 %multiply_add_fusion = (f32[8,4,8,2048]{3,0,1,2:T(8,128)S(1)}, f32[8,4,8,2048]{3,0,1,2:T(8,128)}) fusion(f32[8,4,8,2048]{3,0,1,2:T(8,128)} %bitcast.659, f32[8,4,8,2048]{3,0,1,2:T(8,128)} %bitcast.660, f32[8,4,2048]{2,0,1:T(8,128)S(1)} %bitcast.665, f32[8,4,2048]{2,0,1:T(8,128)S(1)} %bitcast.666), kind=kLoop, calls=%fused_computation.25 | loop fusion | flops 1572864 | bytes 8912896 | tf_op jit(solution)/shard_map/add | solution.py:138
  154.3 1.7 slice_select_fusion.1
  156.3 26.6 %fusion.2 = f32[2,128,2048]{2,1,0:T(8,128)S(1)} fusion(f32[2048,2048]{1,0:T(8,128)} %param.12, f32[2,16,8,2048]{3,0,1,2:T(2,128)S(1)} %bitcast.653, f32[2,16,8,2048]{3,0,1,2:T(2,128)S(1)} %bitcast.652, f32[2,2048]{1,0:T(2,128)S(1)} %fusion.55), kind=kOutput, calls=%fused_computation.2 | convolution fusion | flops 12885950464 | bytes 23085056 | tf_op jit(solution)/shard_map/kjm,im->kji/dot_general | solution.py:169
  183.2 30.9 %all_to_all.30 = f32[8,2,128,256]{3,2,1,0:T(8,128)S(1)} all-to-all(f32[8,2,128,256]{3,2,1,0:T(8,128)S(1)} %fusion.20), channel_id=1, replica_groups=mesh['lat'=16,'lon'=8] {'lon'}, dimensions={0} | all-to-all | bytes 4194304 | tf_op jit(solution)/shard_map/all_to_all | solution.py:171
  214.1 1.3 copy.625
  (143 shorter events, 10.4 us)
Async XLA Ops:
  1.0 20.0 %collective-permute-start.2 = (f32[16,1,256]{2,1,0:T(1,128)S(1)}, f32[16,1,256]{2,1,0:T(1,128)S(1)}, u32[]{:S(2)}, u32[]{:S(2)}) collective-permute-start(f32[16,1,256]{2,1,0:T(1,128)S(1)} %get-tuple-element.92), channel_id=1, source_target_pairs={{0,8},{8,16},{16,24},{24,32},{32,40},{40,48},{48,56},{56,64},{64,7... | collective-permute-start | bytes 49160 | tf_op jit(solution)/shard_map/ppermute | solution.py:15
  5.9 15.0 %collective-permute-start.3 = (f32[16,1,256]{2,1,0:T(1,128)S(1)}, f32[16,1,256]{2,1,0:T(1,128)S(1)}, u32[]{:S(2)}, u32[]{:S(2)}) collective-permute-start(f32[16,1,256]{2,1,0:T(1,128)S(1)} %get-tuple-element.93), channel_id=1, source_target_pairs={{8,0},{16,8},{24,16},{32,24},{40,32},{48,40},{56,48},{64,56},{72,6... | collective-permute-start | bytes 49160 | tf_op jit(solution)/shard_map/ppermute | solution.py:16
  10.7 10.2 %copy-start.1 = (f32[16,128,256]{2,1,0:T(8,128)S(1)}, f32[16,128,256]{2,1,0:T(8,128)}, u32[]{:S(2)}) copy-start(f32[16,128,256]{2,1,0:T(8,128)} %param.8) | copy-start | bytes 6291460
  10.7 10.2 %copy-start.20 = (f32[128,256]{1,0:T(8,128)S(1)}, f32[128,256]{1,0:T(8,128)}, u32[]{:S(2)}) copy-start(f32[128,256]{1,0:T(8,128)} %param.10) | copy-start | bytes 393220
  10.7 10.2 %copy-start.21 = (f32[128,256]{1,0:T(8,128)S(1)}, f32[128,256]{1,0:T(8,128)}, u32[]{:S(2)}) copy-start(f32[128,256]{1,0:T(8,128)} %param.9) | copy-start | bytes 393220
  10.7 10.3 %copy-start.22 = (f32[256]{0:T(256)S(1)}, f32[256]{0:T(256)}, u32[]{:S(2)}) copy-start(f32[256]{0:T(256)} %param.11) | copy-start | bytes 3076
  12.5 6.3 %collective-permute-start = (f32[16,128,1]{1,0,2:T(8,128)S(1)}, f32[16,128,1]{1,0,2:T(8,128)S(1)}, u32[]{:S(2)}, u32[]{:S(2)}) collective-permute-start(f32[16,128,1]{1,0,2:T(8,128)S(1)} %copy.147), channel_id=1, source_target_pairs={{0,1},{1,2},{2,3},{3,4},{4,5},{5,6},{6,7},{7,0},{8,9},{9,10},{10,1... | collective-permute-start | bytes 24584 | tf_op jit(solution)/shard_map/ppermute | solution.py:15
  15.6 4.0 %collective-permute-start.1 = (f32[16,128,1]{1,0,2:T(8,128)S(1)}, f32[16,128,1]{1,0,2:T(8,128)S(1)}, u32[]{:S(2)}, u32[]{:S(2)}) collective-permute-start(f32[16,128,1]{1,0,2:T(8,128)S(1)} %copy.148), channel_id=1, source_target_pairs={{1,0},{2,1},{3,2},{4,3},{5,4},{6,5},{7,6},{0,7},{9,8},{10,9},{11,1... | collective-permute-start | bytes 24584 | tf_op jit(solution)/shard_map/ppermute | solution.py:16
  25.0 34.8 %all-to-all-start = ((f32[16,128,256]{2,1,0:T(8,128)}), f32[16,128,256]{2,1,0:T(8,128)S(1)}, u32[]{:S(2)}, u32[]{:S(2)}) async-start(f32[16,128,256]{2,1,0:T(8,128)} %fusion.7), calls=%async_computation | async-start | bytes 4194304 | tf_op jit(solution)/shard_map/all_to_all | solution.py:155
  64.0 17.2 %copy-start.3 = (f32[2,16,8,2048]{3,2,1,0:T(8,128)S(1)}, f32[2,16,8,2048]{3,2,1,0:T(8,128)}, u32[]{:S(2)}) copy-start(f32[2,16,8,2048]{3,2,1,0:T(8,128)} %negate_bitcast_fusion) | copy-start | bytes 6291460
  84.5 3.4 %copy-start.4 = (f32[2,16,1,2048]{3,2,1,0:T(1,128)}, f32[2,16,1,2048]{3,2,1,0:T(1,128)S(1)}, u32[]{:S(2)}) copy-start(f32[2,16,1,2048]{3,2,1,0:T(1,128)S(1)} %get-tuple-element.189) | copy-start | bytes 786436
  84.5 3.4 %copy-start.6 = (f32[2,16,1,2048]{3,2,1,0:T(1,128)}, f32[2,16,1,2048]{3,2,1,0:T(1,128)S(1)}, u32[]{:S(2)}) copy-start(f32[2,16,1,2048]{3,2,1,0:T(1,128)S(1)} %get-tuple-element.85) | copy-start | bytes 786436
  84.5 3.4 %copy-start.8 = (f32[2,16,1,2048]{3,2,1,0:T(1,128)}, f32[2,16,1,2048]{3,2,1,0:T(1,128)S(1)}, u32[]{:S(2)}) copy-start(f32[2,16,1,2048]{3,2,1,0:T(1,128)S(1)} %get-tuple-element.186) | copy-start | bytes 786436
  85.7 2.8 %copy-start.13 = (f32[2,16,2048]{2,0,1:T(2,128)S(1)}, f32[2,16,2048]{2,0,1:T(2,128)}, u32[]{:S(2)}) copy-start(f32[2,16,2048]{2,0,1:T(2,128)} %constant_dynamic-update-slice_fusion.29) | copy-start | bytes 786436
  87.9 1.2 copy-start.10
  89.1 1.1 copy-start.14
  89.4 0.7 copy-start.11
  91.1 22.0 %all-to-all-start.1 = ((f32[16,4,2048]{2,1,0:T(4,128)}), f32[16,4,2048]{2,1,0:T(4,128)}, u32[]{:S(2)}, u32[]{:S(2)}) async-start(f32[16,4,2048]{2,1,0:T(4,128)} %broadcast_in_dim.48), calls=%async_computation.1 | async-start | bytes 1048576 | tf_op jit(solution)/shard_map/all_to_all | solution.py:23
  97.9 3.2 %copy-start.7 = (f32[2,16,1,2048]{3,2,1,0:T(1,128)S(1)}, f32[2,16,1,2048]{3,2,1,0:T(1,128)}, u32[]{:S(2)}) copy-start(f32[2,16,1,2048]{3,2,1,0:T(1,128)} %copy-done.6) | copy-start | bytes 786436
  97.9 3.1 %copy-start.9 = (f32[2,16,1,2048]{3,2,1,0:T(1,128)S(1)}, f32[2,16,1,2048]{3,2,1,0:T(1,128)}, u32[]{:S(2)}) copy-start(f32[2,16,1,2048]{3,2,1,0:T(1,128)} %copy-done.8) | copy-start | bytes 786436
  104.3 3.1 %copy-start.5 = (f32[2,16,1,2048]{3,2,1,0:T(1,128)S(1)}, f32[2,16,1,2048]{3,2,1,0:T(1,128)}, u32[]{:S(2)}) copy-start(f32[2,16,1,2048]{3,2,1,0:T(1,128)} %copy-done.4) | copy-start | bytes 786436
  106.0 2.9 %copy-start.12 = (f32[2,16,2048]{2,0,1:T(2,128)S(1)}, f32[2,16,2048]{2,0,1:T(2,128)}, u32[]{:S(2)}) copy-start(f32[2,16,2048]{2,0,1:T(2,128)} %copy-done.11) | copy-start | bytes 786436
  106.0 2.9 %copy-start.15 = (f32[2,16,2048]{2,0,1:T(2,128)S(1)}, f32[2,16,2048]{2,0,1:T(2,128)}, u32[]{:S(2)}) copy-start(f32[2,16,2048]{2,0,1:T(2,128)} %copy-done.14) | copy-start | bytes 786436
  113.1 2.0 copy-start.2
  130.1 0.7 copy-start.16
  130.8 0.7 copy-start.18
  132.4 21.9 %all-to-all-start.2 = ((f32[16,4,2048]{2,1,0:T(4,128)}), f32[16,4,2048]{2,1,0:T(4,128)}, u32[]{:S(2)}, u32[]{:S(2)}) async-start(f32[16,4,2048]{2,1,0:T(4,128)} %broadcast_in_dim.52), calls=%async_computation.2 | async-start | bytes 1048576 | tf_op jit(solution)/shard_map/all_to_all | solution.py:23
  145.6 4.5 %copy-start.17 = (f32[2,16,2048]{2,0,1:T(2,128)S(1)}, f32[2,16,2048]{2,0,1:T(2,128)}, u32[]{:S(2)}) copy-start(f32[2,16,2048]{2,0,1:T(2,128)} %copy-done.16) | copy-start | bytes 786436
  145.6 4.5 %copy-start.19 = (f32[2,16,2048]{2,0,1:T(2,128)S(1)}, f32[2,16,2048]{2,0,1:T(2,128)}, u32[]{:S(2)}) copy-start(f32[2,16,2048]{2,0,1:T(2,128)} %copy-done.18) | copy-start | bytes 786436
  154.3 2.1 copy-start
